TPU v7x, 32 devices: a whole 2x2x4 slice. The times are simulated.
32 devices in a mesh: rows: 8 (over y, x, core), cols: 4 (over z).
Axes of the slice: x: 2, y: 2, z: 4, core: 2. Of those that a mesh axis runs over, the one named last changes fastest.
Arguments:
- guidance: float32 [3, 1024, 12288], P(None, 'rows', 'cols'), may hold values from -8 to 8
- initial: float32 [3, 1024, 12288], P(None, 'rows', 'cols'), may hold values from -6 to 6
- labels: int32 [1024, 12288], P('rows', 'cols'), may hold values from 0 to 5
- dirichlet: int32 [1024, 12288], P('rows', 'cols'), may hold values 0 or 1
Outputs:
- blended: float32 [3, 1024, 12288], P(None, 'rows', 'cols')
- residual: float32 [3, 1024, 12288], P(None, 'rows', 'cols')
All inputs are finite; a program needn't handle non-finite values. No bound on the sum of `dirichlet` on one device may be relied on, other than what follows from the above.
Results may differ from a plain program's by a relative error of at most 0.0003.
Values sent between devices are 32-bit elements; how exact they have to be, the bound alone decides.
No kernel may reach another device: no remote copies, remote signals or barrier semaphores. Data moves between devices by JAX's collectives and lax.ppermute only.
A program may use at most 128 MiB of HBM per device.

v0:
```python
import jax
import jax.numpy as jnp
from jax import lax
from jax.sharding import PartitionSpec as P

ITERS = 3


SCREEN = 0.1
SEAM_WEIGHT = 0.5


def with_halo(cells, sides, width):
    for axis, dim in sides:
        count = lax.axis_size(axis)
        ends = count - 1
        head = lax.slice_in_dim(cells, 0, width, axis=dim)
        tail = lax.slice_in_dim(cells, cells.shape[dim] - width, cells.shape[dim], axis=dim)
        cells = jnp.concatenate(
            [
                lax.ppermute(tail, axis, [(i, (i + 1) % count) for i in range(ends)]),
                cells,
                lax.ppermute(head, axis, [((i + 1) % count, i) for i in range(ends)]),
            ],
            axis=dim,
        )
    return cells


def edge_weights(labels):
    padded = with_halo(labels + 1, (("rows", 0), ("cols", 1)), 1)
    center = padded[1:-1, 1:-1]
    sides = [padded[2:, 1:-1], padded[:-2, 1:-1], padded[1:-1, 2:], padded[1:-1, :-2]]
    return [jnp.where(side == center, 1.0, SEAM_WEIGHT).astype(jnp.float32) for side in sides]


def operate(field, weights):
    padded = with_halo(field, (("rows", 1), ("cols", 2)), 1)
    sides = [padded[:, 2:, 1:-1], padded[:, :-2, 1:-1], padded[:, 1:-1, 2:], padded[:, 1:-1, :-2]]
    total = SCREEN * field
    for weight, side in zip(weights, sides):
        total = total + weight * (field - side)
    return total


def paired_sums(residual, applied):
    return lax.psum(
        (jnp.sum(residual * residual, axis=(1, 2)), jnp.sum(residual * applied, axis=(1, 2))),
        ("rows", "cols"),
    )


def widen(vector):
    return vector[:, None, None]


def on_device(guidance, initial, labels, dirichlet):
    free_cells = (1 - dirichlet).astype(jnp.float32)
    weights = edge_weights(labels)
    residual = free_cells * (guidance - operate(initial, weights))
    blended = initial
    applied = free_cells * operate(residual, weights)
    norm_now, product = paired_sums(residual, applied)
    step_size = norm_now / product
    direction = residual
    along = applied
    for turn_index in range(ITERS):
        blended = blended + widen(step_size) * direction
        residual = residual - widen(step_size) * along
        if turn_index + 1 < ITERS:
            applied = free_cells * operate(residual, weights)
            norm_next, product = paired_sums(residual, applied)
            ratio = norm_next / norm_now
            step_size = norm_next / (product - ratio * norm_next / step_size)
            direction = residual + widen(ratio) * direction
            along = applied + widen(ratio) * along
            norm_now = norm_next
    return (blended, residual)


def solution(mesh):
    in_specs = (
        P(None, "rows", "cols"),
        P(None, "rows", "cols"),
        P("rows", "cols"),
        P("rows", "cols"),
    )
    out_specs = (P(None, "rows", "cols"), P(None, "rows", "cols"))
    return jax.shard_map(
        on_device, mesh=mesh, in_specs=in_specs, out_specs=out_specs, check_vma=False
    )
```

profile of v0, /device:TPU:0, one launch (start us, length us, event | category | flops | bytes accessed | tf_op | source)
XLA Modules:
  0.0 294.7 jit_solution(16057997189948095949)
XLA Ops:
  3.3 3.0 %collective-permute-start.3 = (f32[3,1,3072]{2,1,0:T(1,128)S(1)}, f32[3,1,3072]{2,1,0:T(1,128)S(1)}, u32[]{:S(2)}, u32[]{:S(2)}) collective-permute-start(f32[3,1,3072]{2,1,0:T(1,128)S(1)} %get-tuple-element.35), channel_id=1, source_target_pairs={{0,4},{4,8},{8,12},{12,16},{16,20},{20,24},{24,28},{1,5},{5,9},{9,... | collective-permute-start | bytes 110600 | tf_op jit(solution)/shard_map/ppermute | solution.py:21
  9.2 5.1 %collective-permute-start.2 = (s32[1,3072]{1,0:T(1,128)S(1)}, s32[1,3072]{1,0:T(1,128)S(1)}, u32[]{:S(2)}, u32[]{:S(2)}) collective-permute-start(s32[1,3072]{1,0:T(1,128)S(1)} %get-tuple-element.43), channel_id=1, source_target_pairs={{0,4},{4,8},{8,12},{12,16},{16,20},{20,24},{24,28},{1,5},{5,9},{9,... | collective-permute-start | bytes 36872 | tf_op jit(solution)/shard_map/ppermute | solution.py:21
  17.3 4.5 %collective-permute-start.6 = (s32[130,1]{1,0:T(8,128)S(1)}, s32[130,1]{1,0:T(8,128)S(1)}, u32[]{:S(2)}, u32[]{:S(2)}) collective-permute-start(s32[130,1]{1,0:T(8,128)S(1)} %get-tuple-element.40), channel_id=1, source_target_pairs={{0,1},{1,2},{2,3},{4,5},{5,6},{6,7},{8,9},{9,10},{10,11},{12,13},{... | collective-permute-start | bytes 1568 | tf_op jit(solution)/shard_map/ppermute | solution.py:21
  22.1 3.5 %collective-permute-start.7 = (f32[3,130,1]{2,1,0:T(8,128)S(1)}, f32[3,130,1]{2,1,0:T(8,128)S(1)}, u32[]{:S(2)}, u32[]{:S(2)}) collective-permute-start(f32[3,130,1]{2,1,0:T(8,128)S(1)} %get-tuple-element.28), channel_id=1, source_target_pairs={{0,1},{1,2},{2,3},{4,5},{5,6},{6,7},{8,9},{9,10},{10,11},{12,13},{... | collective-permute-start | bytes 4688 | tf_op jit(solution)/shard_map/ppermute | solution.py:21
  30.9 4.5 %collective-permute-done.5 = f32[3,130,1]{2,1,0:T(8,128)S(1)} collective-permute-done((f32[3,130,1]{2,1,0:T(8,128)S(1)}, f32[3,130,1]{2,1,0:T(8,128)S(1)}, u32[]{:S(2)}, u32[]{:S(2)}) %collective-permute-start.5) | collective-permute-done | bytes 1592 | tf_op jit(solution)/shard_map/ppermute | solution.py:23
  35.4 8.2 %fusion.43 = f32[3,128,3072]{2,1,0:T(8,128)S(1)} fusion(f32[3,128,3072]{2,1,0:T(8,128)} %param.4, f32[3,128,3072]{2,1,0:T(8,128)S(1)} %copy-done.20, f32[3,130,1]{2,1,0:T(8,128)S(1)} %collective-permute-done.7, f32[3,1,3072]{2,1,0:T(1,128)S(1)} %collective-permute-done.1, f32[3,1,3072]{2,1,0:T(1,128)S(1)} %collective-permute-done.3, ...), kind=kLoop, calls=%fused_computation.68 | loop fusion | flops 27131904 | bytes 22096944 | tf_op jit(solution)/shard_map/mul | solution.py:60
  49.1 3.5 %collective-permute-start.11 = (f32[3,130,1]{2,1,0:T(8,128)S(1)}, f32[3,130,1]{2,1,0:T(8,128)S(1)}, u32[]{:S(2)}, u32[]{:S(2)}) collective-permute-start(f32[3,130,1]{2,1,0:T(8,128)S(1)} %get-tuple-element.26), channel_id=1, source_target_pairs={{0,1},{1,2},{2,3},{4,5},{5,6},{6,7},{8,9},{9,10},{10,11},{12,13},{... | collective-permute-start | bytes 4688 | tf_op jit(solution)/shard_map/ppermute | solution.py:21
  56.1 4.7 %collective-permute-done.10 = f32[3,130,1]{2,1,0:T(8,128)S(1)} collective-permute-done((f32[3,130,1]{2,1,0:T(8,128)S(1)}, f32[3,130,1]{2,1,0:T(8,128)S(1)}, u32[]{:S(2)}, u32[]{:S(2)}) %collective-permute-start.10) | collective-permute-done | bytes 1592 | tf_op jit(solution)/shard_map/ppermute | solution.py:23
  60.8 12.9 %multiply_reduce_fusion.4 = (f32[3]{0:T(128)S(1)}, f32[3]{0:T(128)S(1)}, f32[3,128,3072]{2,1,0:T(8,128)}) fusion(f32[3,128,3072]{2,1,0:T(8,128)S(1)} %fusion.43, f32[3,1,3072]{2,1,0:T(1,128)S(1)} %collective-permute-done.8, f32[3,1,3072]{2,1,0:T(1,128)S(1)} %collective-permute-done.9, f32[3,130,1]{2,1,0:T(8,128)S(1)} %collective-permute-done.11, ...), kind=kLoop, calls=%fused_computation.94 | loop fusion | flops 30670840 | bytes 17378376 | tf_op jit(solution)/shard_map/reduce_sum | solution.py:48
  73.7 42.5 %all-reduce.2 = (f32[3]{0:T(128)S(1)}, f32[3]{0:T(128)S(1)}) all-reduce(f32[3]{0:T(128)S(1)} %get-tuple-element.7, f32[3]{0:T(128)S(1)} %get-tuple-element.6), channel_id=1, replica_groups=mesh['rows'=8,'cols'=4] {'rows','cols'}, use_global_device_ids=true, to_apply=%region_1.2 | all-reduce | flops 6 | bytes 48 | tf_op jit(solution)/shard_map/psum | solution.py:47
  116.2 5.1 %multiply_subtract_fusion.2 = f32[3,128,3072]{2,1,0:T(8,128)S(1)} fusion(f32[3,128,3072]{2,1,0:T(8,128)} %copy-done, f32[3,128,3072]{2,1,0:T(8,128)} %get-tuple-element.20, f32[3]{0:T(128)S(1)} %div.21), kind=kLoop, calls=%fused_computation.93 | loop fusion | flops 2359296 | bytes 14155788 | tf_op jit(solution)/shard_map/sub | solution.py:69
  123.0 3.2 %collective-permute-start.13 = (f32[3,1,3072]{2,1,0:T(1,128)S(1)}, f32[3,1,3072]{2,1,0:T(1,128)S(1)}, u32[]{:S(2)}, u32[]{:S(2)}) collective-permute-start(f32[3,1,3072]{2,1,0:T(1,128)S(1)} %get-tuple-element.31), channel_id=1, source_target_pairs={{0,4},{4,8},{8,12},{12,16},{16,20},{20,24},{24,28},{1,5},{5,9},{9,... | collective-permute-start | bytes 110600 | tf_op jit(solution)/shard_map/ppermute | solution.py:21
  127.1 3.8 %collective-permute-start.15 = (f32[3,130,1]{2,1,0:T(8,128)S(1)}, f32[3,130,1]{2,1,0:T(8,128)S(1)}, u32[]{:S(2)}, u32[]{:S(2)}) collective-permute-start(f32[3,130,1]{2,1,0:T(8,128)S(1)} %get-tuple-element.24), channel_id=1, source_target_pairs={{0,1},{1,2},{2,3},{4,5},{5,6},{6,7},{8,9},{9,10},{10,11},{12,13},{... | collective-permute-start | bytes 4688 | tf_op jit(solution)/shard_map/ppermute | solution.py:21
  135.3 4.7 %collective-permute-done.14 = f32[3,130,1]{2,1,0:T(8,128)S(1)} collective-permute-done((f32[3,130,1]{2,1,0:T(8,128)S(1)}, f32[3,130,1]{2,1,0:T(8,128)S(1)}, u32[]{:S(2)}, u32[]{:S(2)}) %collective-permute-start.14) | collective-permute-done | bytes 1592 | tf_op jit(solution)/shard_map/ppermute | solution.py:23
  140.0 12.7 %multiply_reduce_fusion.2 = (f32[3]{0:T(128)S(1)}, f32[3]{0:T(128)S(1)}, f32[3,128,3072]{2,1,0:T(8,128)}) fusion(f32[3,128,3072]{2,1,0:T(8,128)S(1)} %multiply_subtract_fusion.2, f32[3,1,3072]{2,1,0:T(1,128)S(1)} %collective-permute-done.12, f32[3,1,3072]{2,1,0:T(1,128)S(1)} %collective-permute-done.13, f32[3,130,1]{2,1,0:T(8,128)S(1)} %collective-permute-done.15, ...), kind=kLoop, calls=%fused_computation.91 | loop fusion | flops 30670840 | bytes 17378376 | tf_op jit(solution)/shard_map/reduce_sum | solution.py:48
  152.7 41.6 %all-reduce.1 = (f32[3]{0:T(128)S(1)}, f32[3]{0:T(128)S(1)}) all-reduce(f32[3]{0:T(128)S(1)} %get-tuple-element.5, f32[3]{0:T(128)S(1)} %get-tuple-element.4), channel_id=1, replica_groups=mesh['rows'=8,'cols'=4] {'rows','cols'}, use_global_device_ids=true, to_apply=%region_5.6 | all-reduce | flops 6 | bytes 48 | tf_op jit(solution)/shard_map/psum | solution.py:47
  194.3 6.7 %multiply_subtract_fusion.1 = f32[3,128,3072]{2,1,0:T(8,128)S(1)} fusion(f32[3,128,3072]{2,1,0:T(8,128)} %copy-done.1, f32[3]{0:T(128)S(1)} %get-tuple-element.16, f32[3,128,3072]{2,1,0:T(8,128)} %get-tuple-element.19, f32[3,128,3072]{2,1,0:T(8,128)} %get-tuple-element.20, f32[3]{0:T(128)S(1)} %get-tuple-element.18), kind=kLoop, calls=%fused_computation.89 | loop fusion | flops 4718592 | bytes 18874392 | tf_op jit(solution)/shard_map/sub | solution.py:69
  202.7 3.2 %collective-permute-start.17 = (f32[3,1,3072]{2,1,0:T(1,128)S(1)}, f32[3,1,3072]{2,1,0:T(1,128)S(1)}, u32[]{:S(2)}, u32[]{:S(2)}) collective-permute-start(f32[3,1,3072]{2,1,0:T(1,128)S(1)} %get-tuple-element.29), channel_id=1, source_target_pairs={{0,4},{4,8},{8,12},{12,16},{16,20},{20,24},{24,28},{1,5},{5,9},{9,... | collective-permute-start | bytes 110600 | tf_op jit(solution)/shard_map/ppermute | solution.py:21
  206.8 3.3 %collective-permute-start.19 = (f32[3,130,1]{2,1,0:T(8,128)S(1)}, f32[3,130,1]{2,1,0:T(8,128)S(1)}, u32[]{:S(2)}, u32[]{:S(2)}) collective-permute-start(f32[3,130,1]{2,1,0:T(8,128)S(1)} %get-tuple-element.22), channel_id=1, source_target_pairs={{0,1},{1,2},{2,3},{4,5},{5,6},{6,7},{8,9},{9,10},{10,11},{12,13},{... | collective-permute-start | bytes 4688 | tf_op jit(solution)/shard_map/ppermute | solution.py:21
  214.4 4.7 %collective-permute-done.18 = f32[3,130,1]{2,1,0:T(8,128)S(1)} collective-permute-done((f32[3,130,1]{2,1,0:T(8,128)S(1)}, f32[3,130,1]{2,1,0:T(8,128)S(1)}, u32[]{:S(2)}, u32[]{:S(2)}) %collective-permute-start.18) | collective-permute-done | bytes 1592 | tf_op jit(solution)/shard_map/ppermute | solution.py:23
  219.1 11.8 %multiply_reduce_fusion = (f32[3]{0:T(128)S(1)}, f32[3]{0:T(128)S(1)}) fusion(f32[3,128,3072]{2,1,0:T(8,128)S(1)} %multiply_subtract_fusion.1, f32[3,1,3072]{2,1,0:T(1,128)S(1)} %collective-permute-done.16, f32[3,1,3072]{2,1,0:T(1,128)S(1)} %collective-permute-done.17, f32[3,130,1]{2,1,0:T(8,128)S(1)} %collective-permute-done.19, ...), kind=kLoop, calls=%fused_computation.87 | loop fusion | flops 30670840 | bytes 12659784 | tf_op jit(solution)/shard_map/reduce_sum | solution.py:48
  231.0 41.1 %all-reduce = (f32[3]{0:T(128)S(1)}, f32[3]{0:T(128)S(1)}) all-reduce(f32[3]{0:T(128)S(1)} %get-tuple-element.3, f32[3]{0:T(128)S(1)} %get-tuple-element.2), channel_id=1, replica_groups=mesh['rows'=8,'cols'=4] {'rows','cols'}, use_global_device_ids=true, to_apply=%region_9.10 | all-reduce | flops 6 | bytes 48 | tf_op jit(solution)/shard_map/psum | solution.py:47
  272.1 10.2 %multiply_add_fusion = f32[3,128,3072]{2,1,0:T(8,128)} fusion(f32[3,128,3072]{2,1,0:T(8,128)} %copy-done.2, f32[3,128,3072]{2,1,0:T(8,128)} %copy-done.1, f32[3,128,3072]{2,1,0:T(8,128)} %copy-done, f32[3,128,3072]{2,1,0:T(8,128)} %param.5, f32[3]{0:T(128)S(1)} %get-tuple-element.15, f32[3]{0:T(128)S(1)} %get-tuple-element.14, f32[3]{0:T(128)S(1)} %get-tuple-element.18, ...), kind=kLoop, calls=%fused_computation.86 | loop fusion | flops 11796480 | bytes 23593020 | tf_op jit(solution)/shard_map/add | solution.py:68
  284.6 10.1 %multiply_subtract_fusion = f32[3,128,3072]{2,1,0:T(8,128)} fusion(f32[3,128,3072]{2,1,0:T(8,128)S(1)} %copy-done.3, f32[3]{0:T(128)S(1)} %get-tuple-element.15, f32[3]{0:T(128)S(1)} %get-tuple-element.14, f32[3,128,3072]{2,1,0:T(8,128)} %get-tuple-element.19, f32[3,128,3072]{2,1,0:T(8,128)S(1)} %bitcast.1, f32[3]{0:T(128)S(1)} %get-tuple-element.18, ...), kind=kLoop, calls=%fused_computation.85 | loop fusion | flops 33030144 | bytes 26815572 | tf_op jit(solution)/shard_map/sub | solution.py:69
  (90 shorter events, 38.8 us)
Async XLA Ops:
  1.9 20.0 %collective-permute-start.1 = (f32[3,1,3072]{2,1,0:T(1,128)S(1)}, f32[3,1,3072]{2,1,0:T(1,128)S(1)}, u32[]{:S(2)}, u32[]{:S(2)}) collective-permute-start(f32[3,1,3072]{2,1,0:T(1,128)S(1)} %get-tuple-element.36), channel_id=1, source_target_pairs={{4,0},{8,4},{12,8},{16,12},{20,16},{24,20},{28,24},{5,1},{9,5},{13... | collective-permute-start | bytes 110600 | tf_op jit(solution)/shard_map/ppermute | solution.py:23
  3.3 18.6 %collective-permute-start.3 = (f32[3,1,3072]{2,1,0:T(1,128)S(1)}, f32[3,1,3072]{2,1,0:T(1,128)S(1)}, u32[]{:S(2)}, u32[]{:S(2)}) collective-permute-start(f32[3,1,3072]{2,1,0:T(1,128)S(1)} %get-tuple-element.35), channel_id=1, source_target_pairs={{0,4},{4,8},{8,12},{12,16},{16,20},{20,24},{24,28},{1,5},{5,9},{9,... | collective-permute-start | bytes 110600 | tf_op jit(solution)/shard_map/ppermute | solution.py:21
  7.9 8.0 %collective-permute-start = (s32[1,3072]{1,0:T(1,128)S(1)}, s32[1,3072]{1,0:T(1,128)S(1)}, u32[]{:S(2)}, u32[]{:S(2)}) collective-permute-start(s32[1,3072]{1,0:T(1,128)S(1)} %get-tuple-element.44), channel_id=1, source_target_pairs={{4,0},{8,4},{12,8},{16,12},{20,16},{24,20},{28,24},{5,1},{9,5},{13... | collective-permute-start | bytes 36872 | tf_op jit(solution)/shard_map/ppermute | solution.py:23
  9.2 6.7 %collective-permute-start.2 = (s32[1,3072]{1,0:T(1,128)S(1)}, s32[1,3072]{1,0:T(1,128)S(1)}, u32[]{:S(2)}, u32[]{:S(2)}) collective-permute-start(s32[1,3072]{1,0:T(1,128)S(1)} %get-tuple-element.43), channel_id=1, source_target_pairs={{0,4},{4,8},{8,12},{12,16},{16,20},{20,24},{24,28},{1,5},{5,9},{9,... | collective-permute-start | bytes 36872 | tf_op jit(solution)/shard_map/ppermute | solution.py:21
  16.0 10.8 %collective-permute-start.4 = (s32[130,1]{1,0:T(8,128)S(1)}, s32[130,1]{1,0:T(8,128)S(1)}, u32[]{:S(2)}, u32[]{:S(2)}) collective-permute-start(s32[130,1]{1,0:T(8,128)S(1)} %get-tuple-element.39), channel_id=1, source_target_pairs={{1,0},{2,1},{3,2},{5,4},{6,5},{7,6},{9,8},{10,9},{11,10},{13,12},{... | collective-permute-start | bytes 1568 | tf_op jit(solution)/shard_map/ppermute | solution.py:23
  17.3 9.5 %collective-permute-start.6 = (s32[130,1]{1,0:T(8,128)S(1)}, s32[130,1]{1,0:T(8,128)S(1)}, u32[]{:S(2)}, u32[]{:S(2)}) collective-permute-start(s32[130,1]{1,0:T(8,128)S(1)} %get-tuple-element.40), channel_id=1, source_target_pairs={{0,1},{1,2},{2,3},{4,5},{5,6},{6,7},{8,9},{9,10},{10,11},{12,13},{... | collective-permute-start | bytes 1568 | tf_op jit(solution)/shard_map/ppermute | solution.py:21
  22.1 8.8 %collective-permute-start.7 = (f32[3,130,1]{2,1,0:T(8,128)S(1)}, f32[3,130,1]{2,1,0:T(8,128)S(1)}, u32[]{:S(2)}, u32[]{:S(2)}) collective-permute-start(f32[3,130,1]{2,1,0:T(8,128)S(1)} %get-tuple-element.28), channel_id=1, source_target_pairs={{0,1},{1,2},{2,3},{4,5},{5,6},{6,7},{8,9},{9,10},{10,11},{12,13},{... | collective-permute-start | bytes 4688 | tf_op jit(solution)/shard_map/ppermute | solution.py:21
  25.6 9.9 %collective-permute-start.5 = (f32[3,130,1]{2,1,0:T(8,128)S(1)}, f32[3,130,1]{2,1,0:T(8,128)S(1)}, u32[]{:S(2)}, u32[]{:S(2)}) collective-permute-start(f32[3,130,1]{2,1,0:T(8,128)S(1)} %get-tuple-element.27), channel_id=1, source_target_pairs={{1,0},{2,1},{3,2},{5,4},{6,5},{7,6},{9,8},{10,9},{11,10},{13,12},{... | collective-permute-start | bytes 4688 | tf_op jit(solution)/shard_map/ppermute | solution.py:23
  28.9 31.8 %copy-start.4 = (f32[128,3072]{1,0:T(8,128)}, f32[128,3072]{1,0:T(8,128)S(1)}, u32[]{:S(2)}) copy-start(f32[128,3072]{1,0:T(8,128)S(1)} %get-tuple-element.37) | copy-start | bytes 4718596
  28.9 31.8 %copy-start.8 = (f32[128,3072]{1,0:T(8,128)}, f32[128,3072]{1,0:T(8,128)S(1)}, u32[]{:S(2)}) copy-start(f32[128,3072]{1,0:T(8,128)S(1)} %get-tuple-element.38) | copy-start | bytes 4718596
  28.9 31.8 %copy-start.12 = (f32[128,3072]{1,0:T(8,128)}, f32[128,3072]{1,0:T(8,128)S(1)}, u32[]{:S(2)}) copy-start(f32[128,3072]{1,0:T(8,128)S(1)} %get-tuple-element.41) | copy-start | bytes 4718596
  43.8 4.3 %collective-permute-start.8 = (f32[3,1,3072]{2,1,0:T(1,128)S(1)}, f32[3,1,3072]{2,1,0:T(1,128)S(1)}, u32[]{:S(2)}, u32[]{:S(2)}) collective-permute-start(f32[3,1,3072]{2,1,0:T(1,128)S(1)} %get-tuple-element.34), channel_id=1, source_target_pairs={{4,0},{8,4},{12,8},{16,12},{20,16},{24,20},{28,24},{5,1},{9,5},{13... | collective-permute-start | bytes 110600 | tf_op jit(solution)/shard_map/ppermute | solution.py:23
  45.1 3.9 %collective-permute-start.9 = (f32[3,1,3072]{2,1,0:T(1,128)S(1)}, f32[3,1,3072]{2,1,0:T(1,128)S(1)}, u32[]{:S(2)}, u32[]{:S(2)}) collective-permute-start(f32[3,1,3072]{2,1,0:T(1,128)S(1)} %get-tuple-element.33), channel_id=1, source_target_pairs={{0,4},{4,8},{8,12},{12,16},{16,20},{20,24},{24,28},{1,5},{5,9},{9,... | collective-permute-start | bytes 110600 | tf_op jit(solution)/shard_map/ppermute | solution.py:21
  49.1 7.0 %collective-permute-start.11 = (f32[3,130,1]{2,1,0:T(8,128)S(1)}, f32[3,130,1]{2,1,0:T(8,128)S(1)}, u32[]{:S(2)}, u32[]{:S(2)}) collective-permute-start(f32[3,130,1]{2,1,0:T(8,128)S(1)} %get-tuple-element.26), channel_id=1, source_target_pairs={{0,1},{1,2},{2,3},{4,5},{5,6},{6,7},{8,9},{9,10},{10,11},{12,13},{... | collective-permute-start | bytes 4688 | tf_op jit(solution)/shard_map/ppermute | solution.py:21
  52.6 8.2 %collective-permute-start.10 = (f32[3,130,1]{2,1,0:T(8,128)S(1)}, f32[3,130,1]{2,1,0:T(8,128)S(1)}, u32[]{:S(2)}, u32[]{:S(2)}) collective-permute-start(f32[3,130,1]{2,1,0:T(8,128)S(1)} %get-tuple-element.25), channel_id=1, source_target_pairs={{1,0},{2,1},{3,2},{5,4},{6,5},{7,6},{9,8},{10,9},{11,10},{13,12},{... | collective-permute-start | bytes 4688 | tf_op jit(solution)/shard_map/ppermute | solution.py:23
  121.4 4.7 %collective-permute-start.12 = (f32[3,1,3072]{2,1,0:T(1,128)S(1)}, f32[3,1,3072]{2,1,0:T(1,128)S(1)}, u32[]{:S(2)}, u32[]{:S(2)}) collective-permute-start(f32[3,1,3072]{2,1,0:T(1,128)S(1)} %get-tuple-element.32), channel_id=1, source_target_pairs={{4,0},{8,4},{12,8},{16,12},{20,16},{24,20},{28,24},{5,1},{9,5},{13... | collective-permute-start | bytes 110600 | tf_op jit(solution)/shard_map/ppermute | solution.py:23
  123.0 4.0 %collective-permute-start.13 = (f32[3,1,3072]{2,1,0:T(1,128)S(1)}, f32[3,1,3072]{2,1,0:T(1,128)S(1)}, u32[]{:S(2)}, u32[]{:S(2)}) collective-permute-start(f32[3,1,3072]{2,1,0:T(1,128)S(1)} %get-tuple-element.31), channel_id=1, source_target_pairs={{0,4},{4,8},{8,12},{12,16},{16,20},{20,24},{24,28},{1,5},{5,9},{9,... | collective-permute-start | bytes 110600 | tf_op jit(solution)/shard_map/ppermute | solution.py:21
  127.1 8.1 %collective-permute-start.15 = (f32[3,130,1]{2,1,0:T(8,128)S(1)}, f32[3,130,1]{2,1,0:T(8,128)S(1)}, u32[]{:S(2)}, u32[]{:S(2)}) collective-permute-start(f32[3,130,1]{2,1,0:T(8,128)S(1)} %get-tuple-element.24), channel_id=1, source_target_pairs={{0,1},{1,2},{2,3},{4,5},{5,6},{6,7},{8,9},{9,10},{10,11},{12,13},{... | collective-permute-start | bytes 4688 | tf_op jit(solution)/shard_map/ppermute | solution.py:21
  131.0 9.0 %collective-permute-start.14 = (f32[3,130,1]{2,1,0:T(8,128)S(1)}, f32[3,130,1]{2,1,0:T(8,128)S(1)}, u32[]{:S(2)}, u32[]{:S(2)}) collective-permute-start(f32[3,130,1]{2,1,0:T(8,128)S(1)} %get-tuple-element.23), channel_id=1, source_target_pairs={{1,0},{2,1},{3,2},{5,4},{6,5},{7,6},{9,8},{10,9},{11,10},{13,12},{... | collective-permute-start | bytes 4688 | tf_op jit(solution)/shard_map/ppermute | solution.py:23
  201.1 4.7 %collective-permute-start.16 = (f32[3,1,3072]{2,1,0:T(1,128)S(1)}, f32[3,1,3072]{2,1,0:T(1,128)S(1)}, u32[]{:S(2)}, u32[]{:S(2)}) collective-permute-start(f32[3,1,3072]{2,1,0:T(1,128)S(1)} %get-tuple-element.30), channel_id=1, source_target_pairs={{4,0},{8,4},{12,8},{16,12},{20,16},{24,20},{28,24},{5,1},{9,5},{13... | collective-permute-start | bytes 110600 | tf_op jit(solution)/shard_map/ppermute | solution.py:23
  202.7 4.0 %collective-permute-start.17 = (f32[3,1,3072]{2,1,0:T(1,128)S(1)}, f32[3,1,3072]{2,1,0:T(1,128)S(1)}, u32[]{:S(2)}, u32[]{:S(2)}) collective-permute-start(f32[3,1,3072]{2,1,0:T(1,128)S(1)} %get-tuple-element.29), channel_id=1, source_target_pairs={{0,4},{4,8},{8,12},{12,16},{16,20},{20,24},{24,28},{1,5},{5,9},{9,... | collective-permute-start | bytes 110600 | tf_op jit(solution)/shard_map/ppermute | solution.py:21
  206.8 7.6 %collective-permute-start.19 = (f32[3,130,1]{2,1,0:T(8,128)S(1)}, f32[3,130,1]{2,1,0:T(8,128)S(1)}, u32[]{:S(2)}, u32[]{:S(2)}) collective-permute-start(f32[3,130,1]{2,1,0:T(8,128)S(1)} %get-tuple-element.22), channel_id=1, source_target_pairs={{0,1},{1,2},{2,3},{4,5},{5,6},{6,7},{8,9},{9,10},{10,11},{12,13},{... | collective-permute-start | bytes 4688 | tf_op jit(solution)/shard_map/ppermute | solution.py:21
  210.1 9.0 %collective-permute-start.18 = (f32[3,130,1]{2,1,0:T(8,128)S(1)}, f32[3,130,1]{2,1,0:T(8,128)S(1)}, u32[]{:S(2)}, u32[]{:S(2)}) collective-permute-start(f32[3,130,1]{2,1,0:T(8,128)S(1)} %get-tuple-element.21), channel_id=1, source_target_pairs={{1,0},{2,1},{3,2},{5,4},{6,5},{7,6},{9,8},{10,9},{11,10},{13,12},{... | collective-permute-start | bytes 4688 | tf_op jit(solution)/shard_map/ppermute | solution.py:23
  219.1 63.1 %slice-start = ((s8[4718592]{0:T(1024)(128)(4,1)}), s8[524288]{0:T(1024)(128)(4,1)S(1)}, s32[]{:S(2)}) async-start(s8[4718592]{0:T(1024)(128)(4,1)} %bitcast), calls=%async_computation | async-start | bytes 1048576
  (19 other events, 370.9 us)
where the time goes:
time: 296 us; the launch traced here: 295 us
  blocking collectives  125 us (42%)
  other arithmetic  83.6 us (28%)
  starting transfers between devices  49.8 us (17%)
  waiting for transfers between devices  31.2 us (11%)
  local copies, waits for them, and re-layouts  3.83 us (1%)
    psum x3, blocking collectives, paired_sums(): lax.psum((jnp.sum(residual * residual, axis=(1, 2)), jnp.sum(residual * a...  125 us
    reduce_sum x3, other arithmetic, paired_sums(): jnp.sum(residual * applied, axis=(1, 2))  37.4 us
    ppermute x10, starting transfers between devices, with_halo(): lax.ppermute(tail, axis, [(i, (i + 1) % count) for i in range(ends)])  36.2 us
    sub x3, other arithmetic, on_device(): residual = residual - widen(step_size) * along  22 us
    ppermute x10, waiting for transfers between devices, with_halo(): lax.ppermute(head, axis, [((i + 1) % count, i) for i in range(ends)])  18.6 us
    ppermute x10, starting transfers between devices, with_halo(): lax.ppermute(head, axis, [((i + 1) % count, i) for i in range(ends)])  13.6 us
    ppermute x10, waiting for transfers between devices, with_halo(): lax.ppermute(tail, axis, [(i, (i + 1) % count) for i in range(ends)])  12.6 us
    add x1, other arithmetic, on_device(): blended = blended + widen(step_size) * direction  10.2 us
  transfers between devices with their start and end apart: 20, of which 11 were waited for; matrix products, arithmetic and copies ran while one was open for 2% of the time, Pallas kernels for 0%

commit v1 on v0

v1 whole, which is shorter than its diff:
```python
import functools

import jax
import jax.numpy as jnp
from jax import lax
from jax.experimental import pallas as pl
from jax.experimental.pallas import tpu as pltpu
from jax.sharding import PartitionSpec as P

ITERS = 3
SCREEN = 0.1
SEAM_WEIGHT = 0.5

RIM = ITERS + 1
MOMENTS = 2 * ITERS
LANES = 128
SUBS = 8
HEAD = SUBS


def lane_ids(shape):
    return lax.broadcasted_iota(jnp.int32, shape, len(shape) - 1)


def sub_ids(shape):
    return lax.broadcasted_iota(jnp.int32, shape, len(shape) - 2)


def lane_roll(x, shift):
    shift = shift % LANES
    return pltpu.roll(x, shift, x.ndim - 1) if shift else x


def sub_swap(x):
    return pltpu.roll(x, SUBS // 2, x.ndim - 2)


def pack_cols_kernel(guid, init, lab, dirc, to_left, to_right, gb, xb, lb, db, sem):
    tiles = guid.shape[2] // LANES
    copies = []
    for side, tile in enumerate((0, tiles - 1)):
        at = pl.ds(tile * LANES, LANES)
        copies += [
            pltpu.make_async_copy(init.at[:, :, at], xb.at[side], sem.at[side, 0]),
            pltpu.make_async_copy(guid.at[:, :, at], gb.at[side], sem.at[side, 1]),
            pltpu.make_async_copy(lab.at[:, at], lb.at[side], sem.at[side, 2]),
            pltpu.make_async_copy(dirc.at[:, at], db.at[side], sem.at[side, 3]),
        ]
    for copy in copies:
        copy.start()
    for copy in copies:
        copy.wait()
    ch, rows = guid.shape[0], guid.shape[1]

    def block(b, _):
        at = pl.ds(pl.multiple_of(b * SUBS, SUBS), SUBS)
        lane = lane_ids((SUBS, LANES))
        for side, out in ((0, to_left), (1, to_right)):
            fields = [xb[side, c, at, :] for c in range(ch)] + [gb[side, c, at, :] for c in range(ch)]
            fields += [(lb[side, at, :] + 1).astype(jnp.float32), (1 - db[side, at, :]).astype(jnp.float32)]
            packed = jnp.zeros((SUBS, LANES), jnp.float32)
            for i, field in enumerate(fields):
                moved = lane_roll(field, RIM * i if side == 0 else RIM * i + RIM)
                packed = jnp.where((lane >= RIM * i) & (lane < RIM * (i + 1)), moved, packed)
            out[at, :] = packed
        return 0

    lax.fori_loop(0, rows // SUBS, block, 0)


def rim_tile(from_left, from_right, i):
    lane = lane_ids(from_left.shape)
    right = lane_roll(from_right, -RIM * i)
    left = lane_roll(from_left, LANES - RIM - RIM * i)
    return jnp.where(lane < RIM, right, jnp.where(lane >= LANES - RIM, left, 0.0))


def pack_rows_kernel(guid, init, lab, dirc, from_left, from_right, to_up, to_down, gb, xb, lb, db, sem):
    ch, rows = guid.shape[0], guid.shape[1]
    tiles = guid.shape[2] // LANES
    copies = []
    for side, row in enumerate((0, rows - SUBS)):
        at = pl.ds(row, SUBS)
        copies += [
            pltpu.make_async_copy(init.at[:, at, :], xb.at[side], sem.at[side, 0]),
            pltpu.make_async_copy(guid.at[:, at, :], gb.at[side], sem.at[side, 1]),
            pltpu.make_async_copy(lab.at[at, :], lb.at[side], sem.at[side, 2]),
            pltpu.make_async_copy(dirc.at[at, :], db.at[side], sem.at[side, 3]),
        ]
    for copy in copies:
        copy.start()
    for copy in copies:
        copy.wait()
    sub = sub_ids((SUBS, LANES))

    def put(t, side, fields):
        out = (to_up, to_down)[side]
        for j in range(len(fields) // 2):
            one, two = fields[2 * j], sub_swap(fields[2 * j + 1])
            keep = sub < RIM if side == 0 else sub >= SUBS - RIM
            out[j, t] = jnp.where(keep, one, two)

    def tile(t, _):
        at = pl.ds(pl.multiple_of(t * LANES, LANES), LANES)
        for side in range(2):
            fields = [xb[side, c, :, at] for c in range(ch)] + [gb[side, c, :, at] for c in range(ch)]
            fields += [(lb[side, :, at] + 1).astype(jnp.float32), (1 - db[side, :, at]).astype(jnp.float32)]
            put(t, side, fields)
        return 0

    lax.fori_loop(0, tiles, tile, 0)
    for side, row in enumerate((0, rows - SUBS)):
        left, right = from_left[row : row + SUBS, :], from_right[row : row + SUBS, :]
        put(tiles, side, [rim_tile(left, right, i) for i in range(2 * ch + 2)])


def krylov_kernel(
    guid, init, lab, dirc, from_left, from_right, from_up, from_down, xs, v0, v1, v2, v3, out,
    lb, fb, cc, cn, cs, ce, cw, acc, sem,
):
    ch, rows = guid.shape[0], guid.shape[1]
    tiles = guid.shape[2] // LANES
    blocks = rows // SUBS
    group = next(g for g in (6, 5, 4, 3, 2, 1) if tiles % g == 0)
    lane = lane_ids((SUBS, LANES))
    sub = sub_ids((SUBS, LANES))

    def fetch(t):
        src = pl.ds(pl.multiple_of(t * LANES, LANES), LANES)
        dst = pl.ds(HEAD, rows)
        return (
            pltpu.make_async_copy(init.at[:, :, src], xs.at[:, t, dst, :], sem.at[0, t]),
            pltpu.make_async_copy(guid.at[:, :, src], v0.at[:, t, dst, :], sem.at[1, t]),
            pltpu.make_async_copy(lab.at[:, src], lb.at[t, dst, :], sem.at[2, t]),
            pltpu.make_async_copy(dirc.at[:, src], fb.at[t, dst, :], sem.at[3, t]),
        )

    def start(t, _):
        for copy in fetch(t):
            copy.start()
        return 0

    def finish(t, _):
        for copy in fetch(t):
            copy.wait()
        return 0

    lax.fori_loop(0, tiles, start, 0)

    def rim_columns(b, _):
        at = pl.ds(pl.multiple_of(b * SUBS, SUBS), SUBS)
        to = pl.ds(pl.multiple_of(b * SUBS + HEAD, SUBS), SUBS)
        left, right = from_left[at, :], from_right[at, :]
        for c in range(ch):
            xs[c, tiles, to, :] = rim_tile(left, right, c)
            v0[c, tiles, to, :] = rim_tile(left, right, ch + c)
        lb[tiles, to, :] = rim_tile(left, right, 2 * ch).astype(jnp.int32) - 1
        fb[tiles, to, :] = 1 - rim_tile(left, right, 2 * ch + 1).astype(jnp.int32)
        return 0

    lax.fori_loop(0, blocks, rim_columns, 0)
    last = HEAD + rows

    def rim_rows(t, _):
        fields = []
        for j in range(ch + 1):
            up, down = from_up[j, t], from_down[j, t]
            fields.append(jnp.where(sub < RIM, down, up))
            fields.append(sub_swap(jnp.where(sub < RIM, up, down)))
        for to in (0, last):
            to = pl.ds(to, SUBS)
            for c in range(ch):
                xs[c, t, to, :] = fields[c]
                v0[c, t, to, :] = fields[ch + c]
            lb[t, to, :] = fields[2 * ch].astype(jnp.int32) - 1
            fb[t, to, :] = 1 - fields[2 * ch + 1].astype(jnp.int32)
        return 0

    lax.fori_loop(0, tiles + 1, rim_rows, 0)

    def beside(get, t0, n):
        ring = tiles + 1
        first = jnp.where(t0 == 0, ring - 1, t0 - 1)
        after = jnp.where(t0 + n == ring, 0, t0 + n)
        return [get(first)] + [get(t0 + i) for i in range(n)] + [get(after)]

    def east(mid, nxt):
        return lane_roll(jnp.where(lane == 0, nxt, mid), -1)

    def west(prev, mid):
        return lane_roll(jnp.where(lane == LANES - 1, prev, mid), 1)

    def north_south(get, row, rim):
        north, south = get(row - 1, SUBS), get(row + 1, SUBS)
        if rim:
            south = jnp.where(sub == SUBS - 1, get(HEAD, 1), south)
        return north, south

    def weigh(t0, n, row, rim):
        at = pl.ds(row, SUBS)
        ring = beside(lambda t: lb[t, at, :], t0, n)
        for i in range(n):
            t = t0 + i
            mid = ring[i + 1]
            north, south = north_south(lambda r, k, t=t: lb[t, pl.ds(r, k), :], row, rim)
            free = (1 - fb[t, at, :]).astype(jnp.float32)
            half = free * SEAM_WEIGHT
            wn, ws, we, ww = (
                jnp.where(side == mid, free, half)
                for side in (north, south, east(mid, ring[i + 2]), west(ring[i], mid))
            )
            cn[t, at, :], cs[t, at, :], ce[t, at, :], cw[t, at, :] = wn, ws, we, ww
            cc[t, at, :] = free * SCREEN + ((wn + ws) + (we + ww))
            for c in range(ch):
                v0[c, t, at, :] = free * v0[c, t, at, :]

    def apply(src, dst, t0, n, row, rim, sums, minus):
        at = pl.ds(row, SUBS)
        fresh = [[], []]
        for c in range(ch):
            ring = beside(lambda t, c=c: src[c, t, at, :], t0, n)
            squares, products = [], []
            for i in range(n):
                t = t0 + i
                mid = ring[i + 1]
                north, south = north_south(lambda r, k, t=t: src[c, t, pl.ds(r, k), :], row, rim)
                value = cc[t, at, :] * mid - (
                    (cn[t, at, :] * north + cs[t, at, :] * south)
                    + (ce[t, at, :] * east(mid, ring[i + 2]) + cw[t, at, :] * west(ring[i], mid))
                )
                if minus:
                    value = dst[c, t, at, :] - value
                dst[c, t, at, :] = value
                if rim:
                    dst[c, t, 0:SUBS, :] = value
                if sums is not None:
                    squares.append(mid * mid)
                    products.append(mid * value)
            if sums is not None:
                fresh[0].append(functools.reduce(jnp.add, squares))
                fresh[1].append(functools.reduce(jnp.add, products))
        if sums is not None:
            return tuple(s + f for s, f in zip(sums, fresh[0] + fresh[1]))

    def inner(run, carry, wait):
        def column(k, carry):
            if wait:
                lax.fori_loop(jnp.where(k == 0, 0, k * group + 1), jnp.minimum(k * group + group + 1, tiles), finish, 0)

            def body(b, carry):
                return run(k * group, group, pl.multiple_of(b * SUBS + HEAD, SUBS), False, carry)

            return lax.fori_loop(0, blocks, body, carry)

        return lax.fori_loop(0, tiles // group, column, carry)

    def outer(run):
        def column(b, _):
            run(tiles, 1, pl.multiple_of(b * SUBS + HEAD, SUBS), False, None)
            return 0

        def line(t, _):
            run(t, 1, last, True, None)
            return 0

        lax.fori_loop(0, blocks, column, 0)
        lax.fori_loop(0, tiles + 1, line, 0)

    def run_weigh(t0, n, row, rim, carry):
        weigh(t0, n, row, rim)
        return 0

    inner(run_weigh, 0, True)
    outer(run_weigh)

    def run_first(t0, n, row, rim, carry):
        apply(xs, v0, t0, n, row, rim, None, True)
        return 0

    inner(run_first, 0, False)
    outer(run_first)

    zero = jnp.zeros((SUBS, LANES), jnp.float32)
    chain = (v0, v1, v2, v3)
    for s in range(ITERS):
        def run(t0, n, row, rim, carry, s=s):
            return apply(chain[s], chain[s + 1], t0, n, row, rim, carry, False)

        sums = inner(run, (zero,) * (2 * ch), False)
        for i in range(2 * ch):
            acc[2 * ch * s + i] = sums[i]
        if s + 1 < ITERS:
            outer(run)

    count = MOMENTS * ch
    row = jnp.sum(acc[...], axis=1)
    high, low = row, jnp.zeros_like(row)
    for step in (64, 32, 16, 8, 4, 2, 1):
        high, low = pair_add((high, low), (lane_roll(high, step), lane_roll(low, step)))
    ids = sub_ids((count, LANES))
    lanes = lane_ids((count, LANES))
    row = jnp.sum(jnp.where(lanes == ids, high, jnp.where(lanes == ids + LANES // 2, low, 0.0)), axis=0, keepdims=True)
    out[...] = jnp.broadcast_to(row[None], out.shape)


def two_sum(a, b):
    s = a + b
    t = s - a
    return s, (a - (s - t)) + (b - t)


def quick_sum(a, b):
    s = a + b
    return s, b - (s - a)


def halves(a):
    t = 4097.0 * a
    high = t - (t - a)
    return high, a - high


def two_product(a, b):
    p = a * b
    ah, al = halves(a)
    bh, bl = halves(b)
    return p, ((ah * bh - p) + ah * bl + al * bh) + al * bl


def pair_add(a, b):
    s, e = two_sum(a[0], b[0])
    return quick_sum(s, e + (a[1] + b[1]))


def pair_sub(a, b):
    return pair_add(a, (-b[0], -b[1]))


def pair_mul(a, b):
    p, e = two_product(a[0], b[0])
    return quick_sum(p, e + (a[0] * b[1] + a[1] * b[0]))


def pair_scale(a, b):
    p, e = two_product(a[0], b)
    return quick_sum(p, e + a[1] * b)


def galerkin(m):
    scale = 1.0 / m[0][0]
    m = [pair_scale(each, scale) for each in m]

    def minor(a, b, c, d):
        return pair_sub(pair_mul(a, b), pair_mul(c, d))

    d = minor(m[1], m[3], m[2], m[2])
    t = minor(m[1], m[4], m[2], m[3])
    e = minor(m[1], m[5], m[3], m[3])
    z1 = minor(m[1], m[1], m[0], m[2])
    z2 = minor(m[1], m[2], m[0], m[3])
    det = minor(d, e, t, t)[0]
    y2 = minor(d, z2, t, z1)[0] / det
    y1 = minor(e, z1, t, z2)[0] / det
    flat = d[0] <= 1e-11 * (m[1][0] * m[3][0])
    done = flat | (det <= 1e-11 * (d[0] * e[0]))
    y2 = jnp.where(done, 0.0, y2)
    y1 = jnp.where(flat, 0.0, jnp.where(done, z1[0] / d[0], y1))
    rest = pair_sub(m[0], pair_add(pair_scale(m[2], y1), pair_scale(m[3], y2)))
    return rest[0] / m[1][0], y1, y2


def finish_kernel(parts, xs, v0, v1, v2, v3, blended, residual, bb, rb, sem):
    ch, rows = blended.shape[0], blended.shape[1]
    tiles = blended.shape[2] // LANES
    blocks = rows // SUBS
    high = parts[:, 0, :]
    low = lane_roll(high, LANES // 2)
    total = (high, low)
    n = high.shape[0]
    while n > 1:
        n //= 2
        total = pair_add((total[0][:n], total[1][:n]), (total[0][n:], total[1][n:]))
    m = [(lane_roll(total[0], -ch * k), lane_roll(total[1], -ch * k)) for k in range(MOMENTS)]
    y = galerkin(m)
    lanes = lane_ids((1, LANES))
    coef = [
        [jnp.broadcast_to(jnp.sum(jnp.where(lanes == c, each, 0.0), axis=1, keepdims=True), (SUBS, LANES)) for each in y]
        for c in range(ch)
    ]

    def put(t):
        dst = pl.ds(pl.multiple_of(t * LANES, LANES), LANES)
        return (
            pltpu.make_async_copy(bb.at[:, t], blended.at[:, :, dst], sem.at[0, t]),
            pltpu.make_async_copy(rb.at[:, t], residual.at[:, :, dst], sem.at[1, t]),
        )

    def tile(t, _):
        for b in range(blocks):
            at = pl.ds(HEAD + b * SUBS, SUBS)
            to = pl.ds(b * SUBS, SUBS)
            for c in range(ch):
                y0, y1, y2 = coef[c]
                a, p, q, r = v0[c, t, at, :], v1[c, t, at, :], v2[c, t, at, :], v3[c, t, at, :]
                bb[c, t, to, :] = xs[c, t, at, :] + (y0 * a + (y1 * p + y2 * q))
                rb[c, t, to, :] = a - (y0 * p + (y1 * q + y2 * r))
        for copy in put(t):
            copy.start()
        return 0

    def drain(t, _):
        for copy in put(t):
            copy.wait()
        return 0

    lax.fori_loop(0, tiles, tile, 0)
    lax.fori_loop(0, tiles, drain, 0)


ANY = pl.BlockSpec(memory_space=pl.ANY)
VMEM = pl.BlockSpec(memory_space=pltpu.VMEM)


def swap_rims(first, last, axis):
    count = lax.axis_size(axis)
    before = lax.ppermute(last, axis, [(i, i + 1) for i in range(count - 1)])
    after = lax.ppermute(first, axis, [(i + 1, i) for i in range(count - 1)])
    return before, after


def on_device(guidance, initial, labels, dirichlet):
    ch, rows, cols = guidance.shape
    tiles = cols // LANES
    fields = 2 * ch + 2
    f32, i32 = jnp.float32, jnp.int32
    devices = lax.axis_size("rows") * lax.axis_size("cols")

    to_left, to_right = pl.pallas_call(
        pack_cols_kernel,
        out_shape=[jax.ShapeDtypeStruct((rows, LANES), f32)] * 2,
        in_specs=[ANY] * 4,
        out_specs=[VMEM] * 2,
        scratch_shapes=[
            pltpu.VMEM((2, ch, rows, LANES), f32),
            pltpu.VMEM((2, ch, rows, LANES), f32),
            pltpu.VMEM((2, rows, LANES), i32),
            pltpu.VMEM((2, rows, LANES), i32),
            pltpu.SemaphoreType.DMA((2, 4)),
        ],
        name="pack_cols",
    )(guidance, initial, labels, dirichlet)
    from_left, from_right = swap_rims(to_left, to_right, "cols")

    to_up, to_down = pl.pallas_call(
        pack_rows_kernel,
        out_shape=[jax.ShapeDtypeStruct((fields // 2, tiles + 1, SUBS, LANES), f32)] * 2,
        in_specs=[ANY] * 4 + [VMEM] * 2,
        out_specs=[VMEM] * 2,
        scratch_shapes=[
            pltpu.VMEM((2, ch, SUBS, cols), f32),
            pltpu.VMEM((2, ch, SUBS, cols), f32),
            pltpu.VMEM((2, SUBS, cols), i32),
            pltpu.VMEM((2, SUBS, cols), i32),
            pltpu.SemaphoreType.DMA((2, 4)),
        ],
        name="pack_rows",
    )(guidance, initial, labels, dirichlet, from_left, from_right)
    from_up, from_down = swap_rims(to_up, to_down, "rows")

    deep = HEAD + rows + 2 * SUBS
    field = pltpu.VMEM((ch, tiles + 1, deep, LANES), f32)
    plane = (tiles + 1, deep, LANES)
    *fields_of, parts = pl.pallas_call(
        krylov_kernel,
        out_shape=[field] * 5 + [jax.ShapeDtypeStruct((devices, 1, LANES), f32)],
        in_specs=[ANY] * 4 + [VMEM] * 4,
        out_specs=[VMEM] * 6,
        scratch_shapes=[pltpu.VMEM(plane, i32)] * 2
        + [pltpu.VMEM(plane, f32)] * 5
        + [pltpu.VMEM((MOMENTS * ch, SUBS, LANES), f32), pltpu.SemaphoreType.DMA((4, tiles))],
        compiler_params=pltpu.CompilerParams(vmem_limit_bytes=24 << 20),
        name="krylov",
    )(guidance, initial, labels, dirichlet, from_left, from_right, from_up, from_down)

    parts = lax.all_to_all(parts, ("rows", "cols"), 0, 0)

    result = jax.ShapeDtypeStruct((ch, rows, cols), f32)
    return pl.pallas_call(
        finish_kernel,
        out_shape=[result] * 2,
        in_specs=[VMEM] * 6,
        out_specs=[ANY] * 2,
        scratch_shapes=[pltpu.VMEM((ch, tiles, rows, LANES), f32)] * 2 + [pltpu.SemaphoreType.DMA((2, tiles))],
        compiler_params=pltpu.CompilerParams(vmem_limit_bytes=24 << 20),
        name="finish",
    )(parts, *fields_of)


def solution(mesh):
    in_specs = (
        P(None, "rows", "cols"),
        P(None, "rows", "cols"),
        P("rows", "cols"),
        P("rows", "cols"),
    )
    out_specs = (P(None, "rows", "cols"), P(None, "rows", "cols"))

    def step(*args):
        return tuple(on_device(*args))

    return jax.shard_map(step, mesh=mesh, in_specs=in_specs, out_specs=out_specs, check_vma=False)
```

time: 296 us -> 103 us (0.35)
  blocking collectives: 125 us -> 18.3 us
  other arithmetic: 83.6 us -> 0 us
  Pallas kernels: 0 us -> 63.5 us
  starting transfers between devices: 49.8 us -> 8.86 us
  waiting for transfers between devices: 31.2 us -> 9.32 us
    psum x3 -> x0, blocking collectives: 125 us -> none  [paired_sums(): lax.psum((jnp.sum(residual * residual, axis=(1, 2)), jnp.sum(residual * a...]
    pallas_call x0 -> x4, Pallas kernels: none -> 63.5 us  [the longest x1 52.1 us: on_device(): pl.pallas_call(krylov_kernel, out_shape=[field] * 5 + [jax.ShapeDtypeStru...]
    ppermute x20 -> x4, starting transfers between devices: 49.8 us -> 8.86 us  [the longest x2 6.27 us: swap_rims(): before = lax.ppermute(last, axis, [(i, i + 1) for i in range(count - 1)])]
    reduce_sum x3 -> x0, other arithmetic: 37.4 us -> none  [paired_sums(): jnp.sum(residual * applied, axis=(1, 2))]
    sub x3 -> x0, other arithmetic: 22 us -> none  [on_device(): residual = residual - widen(step_size) * along]
    ppermute x20 -> x4, waiting for transfers between devices: 31.2 us -> 9.32 us  [the longest x2 8.18 us: swap_rims(): after = lax.ppermute(first, axis, [(i + 1, i) for i in range(count - 1)])]
    all_to_all x0 -> x1, blocking collectives: none -> 18.3 us  [on_device(): parts = lax.all_to_all(parts, ('rows', 'cols'), 0, 0)]
    add x2 -> x0, other arithmetic: 11.7 us -> none  [the longest x1 10.2 us: on_device(): blended = blended + widen(step_size) * direction]
  transfers between devices with their start and end apart: 20 -> 4, of which waited for: 11 -> 4; matrix products, arithmetic and copies ran while one was open for 2% -> 0% of each run, Pallas kernels for 0% -> 0%
where the time goes in v1:
time: 103 us
  Pallas kernels  63.5 us (62%)
  blocking collectives  18.3 us (18%)
  waiting for transfers between devices  9.32 us (9%)
  starting transfers between devices  8.86 us (9%)
  local copies, waits for them, and re-layouts  2.3 us (2%)
    pallas_call x1, Pallas kernels, on_device(): pl.pallas_call(krylov_kernel, out_shape=[field] * 5 + [jax.ShapeDtypeStru...  52.1 us
    all_to_all x1, blocking collectives, on_device(): parts = lax.all_to_all(parts, ('rows', 'cols'), 0, 0)  18.3 us
    ppermute x2, waiting for transfers between devices, swap_rims(): after = lax.ppermute(first, axis, [(i + 1, i) for i in range(count - 1)])  8.18 us
    ppermute x2, starting transfers between devices, swap_rims(): before = lax.ppermute(last, axis, [(i, i + 1) for i in range(count - 1)])  6.27 us
    pallas_call x1, Pallas kernels, on_device(): pl.pallas_call(finish_kernel, out_shape=[result] * 2, in_specs=[VMEM] * 6...  4.47 us
    pallas_call x1, Pallas kernels, on_device(): pl.pallas_call(pack_rows_kernel, out_shape=[jax.ShapeDtypeStruct((fields...  3.62 us
    pallas_call x1, Pallas kernels, on_device(): pl.pallas_call(pack_cols_kernel, out_shape=[jax.ShapeDtypeStruct((rows, L...  3.35 us
    ppermute x2, starting transfers between devices, swap_rims(): after = lax.ppermute(first, axis, [(i + 1, i) for i in range(count - 1)])  2.58 us
  transfers between devices with their start and end apart: 4, of which 4 were waited for; matrix products, arithmetic and copies ran while one was open for 0% of the time, Pallas kernels for 0%

profile of v1, /device:TPU:0, one launch (start us, length us, event | category | flops | bytes accessed | tf_op | source)
XLA Modules:
  0.0 102.9 jit_solution(3879109685452477878)
XLA Ops:
  0.6 3.3 %pack_cols.1 = (f32[128,128]{1,0:T(8,128)}, f32[128,128]{1,0:T(8,128)}) custom-call(f32[3,128,3072]{2,1,0:T(8,128)} %guid.5, f32[3,128,3072]{2,1,0:T(8,128)} %init.5, s32[128,3072]{1,0:T(8,128)} %lab.5, s32[128,3072]{1,0:T(8,128)} %dirc.5), custom_call_target="tpu_custom_call" | custom-call | tf_op jit(solution)/shard_map/pack_cols/pallas_call | solution.py:438
  4.0 5.0 %collective-permute-start = (f32[128,128]{1,0:T(8,128)}, f32[128,128]{1,0:T(8,128)S(1)}, u32[]{:S(2)}, u32[]{:S(2)}) collective-permute-start(f32[128,128]{1,0:T(8,128)} %get-tuple-element.12), channel_id=1, source_target_pairs={{0,1},{1,2},{2,3},{4,5},{5,6},{6,7},{8,9},{9,10},{10,11},{12,13},{... | collective-permute-start | bytes 196616 | tf_op jit(solution)/shard_map/ppermute | solution.py:426
  8.9 1.3 %collective-permute-start.1 = (f32[128,128]{1,0:T(8,128)}, f32[128,128]{1,0:T(8,128)S(1)}, u32[]{:S(2)}, u32[]{:S(2)}) collective-permute-start(f32[128,128]{1,0:T(8,128)} %get-tuple-element.13), channel_id=1, source_target_pairs={{1,0},{2,1},{3,2},{5,4},{6,5},{7,6},{9,8},{10,9},{11,10},{13,12},{... | collective-permute-start | bytes 196616 | tf_op jit(solution)/shard_map/ppermute | solution.py:427
  10.2 0.9 collective-permute-done.from_left
  11.1 0.0 copy-start
  11.2 4.2 %collective-permute-done.1.from_right = f32[128,128]{1,0:T(8,128)S(1)} collective-permute-done((f32[128,128]{1,0:T(8,128)}, f32[128,128]{1,0:T(8,128)S(1)}, u32[]{:S(2)}, u32[]{:S(2)}) %collective-permute-start.1) | collective-permute-done | bytes 65568 | tf_op jit(solution)/shard_map/ppermute | solution.py:427
  15.3 0.0 copy-done
  15.3 0.0 copy-start.2
  15.3 0.6 copy-done.2
  15.9 3.6 %pack_rows.1 = (f32[4,25,8,128]{3,2,1,0:T(8,128)}, f32[4,25,8,128]{3,2,1,0:T(8,128)}) custom-call(f32[3,128,3072]{2,1,0:T(8,128)} %guid.5, f32[3,128,3072]{2,1,0:T(8,128)} %init.5, s32[128,3072]{1,0:T(8,128)} %lab.5, s32[128,3072]{1,0:T(8,128)} %dirc.5, f32[128,128]{1,0:T(8,128)} %copy-done, f32[128,128]{1,0:T(8,128)} %copy-done.2), custom_call_target="tpu_custom_call" | custom-call | tf_op jit(solution)/shard_map/pack_rows/pallas_call | solution.py:454
  19.6 1.3 %collective-permute-start.2 = (f32[4,25,8,128]{3,2,1,0:T(8,128)}, f32[4,25,8,128]{3,2,1,0:T(8,128)S(1)}, u32[]{:S(2)}, u32[]{:S(2)}) collective-permute-start(f32[4,25,8,128]{3,2,1,0:T(8,128)} %get-tuple-element.14), channel_id=1, source_target_pairs={{0,4},{4,8},{8,12},{12,16},{16,20},{20,24},{24,28},{1,5},{5,9},{9,... | collective-permute-start | bytes 1228808 | tf_op jit(solution)/shard_map/ppermute | solution.py:426
  20.9 1.3 %collective-permute-start.3 = (f32[4,25,8,128]{3,2,1,0:T(8,128)}, f32[4,25,8,128]{3,2,1,0:T(8,128)S(1)}, u32[]{:S(2)}, u32[]{:S(2)}) collective-permute-start(f32[4,25,8,128]{3,2,1,0:T(8,128)} %get-tuple-element.15), channel_id=1, source_target_pairs={{4,0},{8,4},{12,8},{16,12},{20,16},{24,20},{28,24},{5,1},{9,5},{13... | collective-permute-start | bytes 1228808 | tf_op jit(solution)/shard_map/ppermute | solution.py:427
  22.2 0.2 collective-permute-done.2.from_up
  22.4 4.0 %collective-permute-done.3.from_down = f32[4,25,8,128]{3,2,1,0:T(8,128)S(1)} collective-permute-done((f32[4,25,8,128]{3,2,1,0:T(8,128)}, f32[4,25,8,128]{3,2,1,0:T(8,128)S(1)}, u32[]{:S(2)}, u32[]{:S(2)}) %collective-permute-start.3) | collective-permute-done | bytes 409632 | tf_op jit(solution)/shard_map/ppermute | solution.py:427
  26.4 0.0 copy-start.1
  26.4 0.8 copy-done.1
  27.3 0.0 copy-start.3
  27.3 0.8 copy-done.3
  28.1 52.1 %krylov.1 = (f32[3,25,152,128]{3,2,1,0:T(8,128)S(1)}, f32[3,25,152,128]{3,2,1,0:T(8,128)S(1)}, f32[3,25,152,128]{3,2,1,0:T(8,128)S(1)}, f32[3,25,152,128]{3,2,1,...) custom-call(f32[3,128,3072]{2,1,0:T(8,128)} %guid.5, f32[3,128,3072]{2,1,0:T(8,128)} %init.5, ...), custom_call_target="tpu_custom_call" | custom-call | tf_op jit(solution)/shard_map/krylov/pallas_call | solution.py:473
  80.2 18.3 %all_to_all.5.parts = f32[32,1,128]{2,1,0:T(1,128)S(1)} all-to-all(f32[32,1,128]{2,1,0:T(1,128)S(1)} %get-tuple-element.16), channel_id=1, replica_groups=mesh['rows'=8,'cols'=4] {'rows','cols'}, dimensions={0} | all-to-all | bytes 32768 | tf_op jit(solution)/shard_map/all_to_all | solution.py:485
  98.5 4.5 %finish.1 = (f32[3,128,3072]{2,1,0:T(8,128)}, f32[3,128,3072]{2,1,0:T(8,128)}) custom-call(f32[32,1,128]{2,1,0:T(1,128)S(1)} %all_to_all.5.parts, f32[3,25,152,128]{3,2,1,0:T(8,128)S(1)} %get-tuple-element.17.xs, f32[3,25,152,128]{3,2,1,0:T(8,128)S(1)} %get-tuple-element.18.v0, f32[3,25,152,128]{3,2,1,0:T(8,128)S(1)} %get-tuple-element.19.v1, ...), custom_call_target="tpu_custom_call" | custom-call | tf_op jit(solution)/shard_map/finish/pallas_call | solution.py:488
Async XLA Ops:
  4.0 7.2 %collective-permute-start = (f32[128,128]{1,0:T(8,128)}, f32[128,128]{1,0:T(8,128)S(1)}, u32[]{:S(2)}, u32[]{:S(2)}) collective-permute-start(f32[128,128]{1,0:T(8,128)} %get-tuple-element.12), channel_id=1, source_target_pairs={{0,1},{1,2},{2,3},{4,5},{5,6},{6,7},{8,9},{9,10},{10,11},{12,13},{... | collective-permute-start | bytes 196616 | tf_op jit(solution)/shard_map/ppermute | solution.py:426
  8.9 6.4 %collective-permute-start.1 = (f32[128,128]{1,0:T(8,128)}, f32[128,128]{1,0:T(8,128)S(1)}, u32[]{:S(2)}, u32[]{:S(2)}) collective-permute-start(f32[128,128]{1,0:T(8,128)} %get-tuple-element.13), channel_id=1, source_target_pairs={{1,0},{2,1},{3,2},{5,4},{6,5},{7,6},{9,8},{10,9},{11,10},{13,12},{... | collective-permute-start | bytes 196616 | tf_op jit(solution)/shard_map/ppermute | solution.py:427
  11.1 4.2 %copy-start = (f32[128,128]{1,0:T(8,128)}, f32[128,128]{1,0:T(8,128)S(1)}, u32[]{:S(2)}) copy-start(f32[128,128]{1,0:T(8,128)S(1)} %collective-permute-done.from_left) | copy-start | bytes 196612
  15.3 0.6 copy-start.2
  19.6 2.9 %collective-permute-start.2 = (f32[4,25,8,128]{3,2,1,0:T(8,128)}, f32[4,25,8,128]{3,2,1,0:T(8,128)S(1)}, u32[]{:S(2)}, u32[]{:S(2)}) collective-permute-start(f32[4,25,8,128]{3,2,1,0:T(8,128)} %get-tuple-element.14), channel_id=1, source_target_pairs={{0,4},{4,8},{8,12},{12,16},{16,20},{20,24},{24,28},{1,5},{5,9},{9,... | collective-permute-start | bytes 1228808 | tf_op jit(solution)/shard_map/ppermute | solution.py:426
  20.9 5.6 %collective-permute-start.3 = (f32[4,25,8,128]{3,2,1,0:T(8,128)}, f32[4,25,8,128]{3,2,1,0:T(8,128)S(1)}, u32[]{:S(2)}, u32[]{:S(2)}) collective-permute-start(f32[4,25,8,128]{3,2,1,0:T(8,128)} %get-tuple-element.15), channel_id=1, source_target_pairs={{4,0},{8,4},{12,8},{16,12},{20,16},{24,20},{28,24},{5,1},{9,5},{13... | collective-permute-start | bytes 1228808 | tf_op jit(solution)/shard_map/ppermute | solution.py:427
  26.4 0.8 copy-start.1
  27.3 0.8 copy-start.3
